TPU v7x, 256 devices: a whole 4x4x8 slice. The times are simulated.
256 devices in a mesh: blk: 64 (over x_hi, y, z), row: 4 (over x_lo, core).
Axes of the slice: x: 4 (x_hi: 2, x_lo: 2; x = x_hi * 2 + x_lo), y: 4, z: 8, core: 2. Of those that a mesh axis runs over, the one named last changes fastest.
Arguments:
- pool_embeds: bfloat16 [65536, 768], P('blk'), may hold values from -24 to 24
- target_samples: bfloat16 [16384, 768], P(('blk', 'row')), may hold values from -6 to 6
- reference_samples: bfloat16 [16384, 768], P(('blk', 'row')), may hold values from -6 to 6
Outputs:
- log_ratio: float32 [65536], P('blk')
- standardized: float32 [65536], P('blk')
All inputs are finite; a program needn't handle non-finite values.
Results may differ from a plain program's by a relative error of at most 0.0003.
Values may be sent and summed in bfloat16 or wider, within the bound.
No kernel may reach another device: no remote copies, remote signals or barrier semaphores. Data moves between devices by JAX's collectives and lax.ppermute only.
A program may use at most 128 MiB of HBM per device.

v0:
```python
import jax
import jax.numpy as jnp
from jax import lax
from jax.sharding import PartitionSpec as P

KERNEL_GAIN = 30.0


def make_fold(pool_rows):
    pool_norms = jnp.sum(jnp.square(pool_rows.astype(jnp.float32)), axis=1)
    factor = KERNEL_GAIN / pool_rows.shape[1]

    def fold(running, pieces, offset):
        width = pieces[0].shape[0]
        joined = jnp.concatenate([pieces[0], pieces[1]], axis=0)
        joined_norms = jnp.sum(jnp.square(joined.astype(jnp.float32)), axis=1)
        products = jnp.dot(pool_rows, joined.T, preferred_element_type=jnp.float32)
        scores_all = (2.0 * products - pool_norms[:, None] - joined_norms[None, :]) * factor
        result = []
        for member in range(2):
            highest = running[2 * member]
            total = running[2 * member + 1]
            scores = scores_all[:, member * width : (member + 1) * width]
            new_high = jnp.maximum(highest, jnp.max(scores, axis=1))
            new_total = jnp.sum(jnp.exp(scores - new_high[:, None]), axis=1)
            result.append(new_high)
            result.append(new_total)
        return tuple(result)

    return fold


def start_state(count):
    lowest = jnp.full((count,), -1e30, jnp.float32)
    nothing = jnp.zeros((count,), jnp.float32)
    return (lowest, nothing, lowest, nothing)


def body(pool_embeds, target_samples, reference_samples):
    pool_count = pool_embeds.shape[0]
    fold = make_fold(pool_embeds)
    state = fold(
        start_state(pool_count),
        (
            lax.all_gather(target_samples, "blk", axis=0, tiled=True),
            lax.all_gather(reference_samples, "blk", axis=0, tiled=True),
        ),
        jnp.int32(0),
    )
    high_target, high_ref = lax.pmax((state[0], state[2]), "row")
    total_target, total_ref = lax.psum(
        (state[1] * jnp.exp(state[0] - high_target), state[3] * jnp.exp(state[2] - high_ref)), "row"
    )
    log_ratio = high_target + jnp.log(total_target) - (high_ref + jnp.log(total_ref))
    whole_count = pool_count * lax.axis_size("blk")
    mean_value = lax.psum(jnp.sum(log_ratio), "blk") / whole_count
    variance = lax.psum(jnp.sum(jnp.square(log_ratio - mean_value)), "blk") / whole_count
    standardized = (log_ratio - mean_value) / jnp.sqrt(variance + 1e-05)
    return (log_ratio, standardized)


def solution(mesh):
    in_specs = (P("blk", None), P(("blk", "row"), None), P(("blk", "row"), None))
    out_specs = (P("blk"), P("blk"))
    return jax.shard_map(body, mesh=mesh, in_specs=in_specs, out_specs=out_specs, check_vma=False)
```

profile of v0, /device:TPU:32, one launch (start us, length us, event | category | flops | bytes accessed | tf_op | source)
XLA Modules:
  0.0 733.3 jit_solution(2255203302230212441)
XLA Ops:
  7.2 0.0 all-gather.3.cloned.1.call-start
  7.2 0.7 all-gather.3.cloned.1.call-update
  7.9 0.0 all-gather.5.cloned.1.call-start
  7.9 0.7 all-gather.5.cloned.1.call-update
  8.6 1.8 multiply_reduce_fusion.1
  10.4 0.0 copy-start.1
  10.4 141.4 %all-gather.3.cloned.1.call-done = bf16[4096,768]{1,0:T(8,128)(2,1)} async-done(((bf16[64,768]{1,0:T(8,128)(2,1)}), bf16[4096,768]{1,0:T(8,128)(2,1)}) %all-gather.3.cloned.1.call-update) | async-done | bytes 6291472 | tf_op jit(solution)/shard_map/all_gather | solution.py:45
  151.9 5.8 constant_dynamic-update-slice_fusion.1
  157.7 132.4 %all-gather.5.cloned.1.call-done = bf16[4096,768]{1,0:T(8,128)(2,1)} async-done(((bf16[64,768]{1,0:T(8,128)(2,1)}), bf16[4096,768]{1,0:T(8,128)(2,1)}) %all-gather.5.cloned.1.call-update) | async-done | bytes 6291472 | tf_op jit(solution)/shard_map/all_gather | solution.py:46
  290.1 5.8 constant_dynamic-update-slice_fusion
  295.9 7.1 multiply_reduce_fusion
  303.0 0.0 copy-done.1
  303.0 23.5 %multiply_bitcast_fusion = f32[1024,8192]{0,1:T(8,128)} fusion(bf16[8192,768]{1,0:T(8,128)(2,1)} %constant_dynamic-update-slice_fusion, bf16[1024,768]{1,0:T(8,128)(2,1)S(1)} %copy-done.1, f32[8192]{0:T(1024)S(1)} %multiply_reduce_fusion, f32[1024]{0:T(1024)S(1)} %multiply_reduce_fusion.1), kind=kOutput, calls=%fused_computation | convolution fusion | flops 12918456320 | bytes 47747072 | tf_op jit(solution)/shard_map/dot_general | solution.py:17
  326.5 11.7 %slice_reduce_fusion.1 = (f32[1024]{0:T(1024)S(1)}, f32[1024]{0:T(1024)S(1)}) fusion(f32[1024,8192]{0,1:T(8,128)} %multiply_bitcast_fusion), kind=kLoop, calls=%fused_computation.5 | loop fusion | flops 8386560 | bytes 33562624 | tf_op jit(solution)/shard_map/reduce_max | solution.py:24
  338.2 8.6 %copy-done = f32[1024,8192]{0,1:T(8,128)S(1)} copy-done((f32[1024,8192]{0,1:T(8,128)S(1)}, f32[1024,8192]{0,1:T(8,128)}, u32[]{:S(2)}) %copy-start) | copy-done | bytes 33554456
  346.7 4.5 exponential_reduce_fusion.1
  351.2 6.1 all-reduce.1
  357.4 5.9 all-reduce
  363.3 0.6 fusion
  363.9 177.7 %psum.30 = f32[]{:T(128)} all-reduce(f32[]{:T(128)} %get-tuple-element.10), channel_id=1, replica_groups=mesh['blk'=64,'row'=4] {'blk'}, use_global_device_ids=true, to_apply=%region_11.0 | all-reduce | flops 1 | bytes 8 | tf_op jit(solution)/shard_map/psum | solution.py:56
  542.3 0.6 multiply_reduce_fusion.2
  542.9 182.2 %psum.31 = f32[]{:T(128)} all-reduce(f32[]{:T(128)} %multiply_reduce_fusion.2), channel_id=1, replica_groups=mesh['blk'=64,'row'=4] {'blk'}, use_global_device_ids=true, to_apply=%region_13.0 | all-reduce | flops 1 | bytes 8 | tf_op jit(solution)/shard_map/psum | solution.py:57
  725.8 0.6 subtract_divide_fusion
  726.4 0.0 copy-done.2
  (5 shorter events, 0.0 us)
Async XLA Ops:
  7.2 144.7 %all-gather.3.cloned.1.call-start = ((), (), s32[]{:S(2)}) async-start(), calls=%async_computation | async-start | bytes 6389760 | tf_op jit(solution)/shard_map/all_gather | solution.py:45
  7.9 282.2 %all-gather.5.cloned.1.call-start = ((), (), s32[]{:S(2)}) async-start(), calls=%async_computation.1 | async-start | bytes 6389760 | tf_op jit(solution)/shard_map/all_gather | solution.py:46
  10.4 292.6 %copy-start.1 = (bf16[1024,768]{1,0:T(8,128)(2,1)S(1)}, bf16[1024,768]{1,0:T(8,128)(2,1)}, u32[]{:S(2)}) copy-start(bf16[1024,768]{1,0:T(8,128)(2,1)} %param.3) | copy-start | bytes 4718596
  326.5 20.3 %copy-start = (f32[1024,8192]{0,1:T(8,128)S(1)}, f32[1024,8192]{0,1:T(8,128)}, u32[]{:S(2)}) copy-start(f32[1024,8192]{0,1:T(8,128)} %multiply_bitcast_fusion) | copy-start | bytes 100663296
  363.9 362.5 %copy-start.2 = (f32[1024]{0:T(1024)}, f32[1024]{0:T(1024)S(1)}, u32[]{:S(2)}) copy-start(f32[1024]{0:T(1024)S(1)} %get-tuple-element.11) | copy-start | bytes 12292
Sparse Core Ops, SparseCore 0:
  11.7 140.1 all-gather.2
  155.6 134.4 all-gather.4
where the time goes:
time: 734 us; the launch traced here: 733 us
  blocking collectives  372 us (51%)
  waiting for transfers between devices  275 us (37%)
  other arithmetic  26.9 us (4%)
  matrix products  23.5 us (3%)
  local copies, waits for them, and re-layouts  20.2 us (3%)
  between operations  15.5 us (2%)
    psum x1, blocking collectives, body(): lax.psum(jnp.sum(jnp.square(log_ratio - mean_value)), 'blk') / whole_count  182 us
    psum x1, blocking collectives, body(): mean_value = lax.psum(jnp.sum(log_ratio), 'blk') / whole_count  178 us
    all_gather x1, waiting for transfers between devices, body(): lax.all_gather(target_samples, 'blk', axis=0, tiled=True)  141 us
    all_gather x1, waiting for transfers between devices, body(): lax.all_gather(reference_samples, 'blk', axis=0, tiled=True)  132 us
    dot_general x1, matrix products, fold(): products = jnp.dot(pool_rows, joined.T, preferred_element_type=jnp.float32)  23.5 us
  transfers between devices with their start and end apart: 2, of which 2 were waited for; matrix products, arithmetic and copies ran while one was open for 1% of the time, Pallas kernels for 0%

commit v1 on v0

--- a/solution.py
+++ b/solution.py
@@ -42,7 +42,10 @@
     state = fold(
         start_state(pool_count),
         (
-            lax.all_gather(target_samples, "blk", axis=0, tiled=True),
+            jnp.concatenate(
+                lax.all_to_all(jnp.stack([target_samples] * lax.axis_size("blk")), "blk", 0, 0),
+                axis=0,
+            ),
             lax.all_gather(reference_samples, "blk", axis=0, tiled=True),
         ),
         jnp.int32(0),

time: 734 us -> 641 us (0.87)
  waiting for transfers between devices: 275 us -> 176 us
  starting transfers between devices: 0.08 us -> 14.4 us
    all_gather x1 -> x0, waiting for transfers between devices: 141 us -> none  [body(): lax.all_gather(target_samples, 'blk', axis=0, tiled=True)]
    all_gather x1, waiting for transfers between devices: 132 us -> 176 us  [body(): lax.all_gather(reference_samples, 'blk', axis=0, tiled=True)]
    all_to_all x0 -> x1, starting transfers between devices: none -> 14.4 us  [body(): lax.all_to_all(jnp.stack([target_samples] * lax.axis_size('blk')), 'blk',...]
  transfers between devices with their start and end apart: 2 -> 2, of which waited for: 2 -> 1; matrix products, arithmetic and copies ran while one was open for 1% -> 1% of each run, Pallas kernels for 0% -> 0%
where the time goes in v1:
time: 641 us
  blocking collectives  370 us (58%)
  waiting for transfers between devices  176 us (27%)
  other arithmetic  27.9 us (4%)
  matrix products  23.1 us (4%)
  between operations  15.5 us (2%)
  starting transfers between devices  14.4 us (2%)
  local copies, waits for them, and re-layouts  12.9 us (2%)
    psum x1, blocking collectives, body(): lax.psum(jnp.sum(jnp.square(log_ratio - mean_value)), 'blk') / whole_count  182 us
    psum x1, blocking collectives, body(): mean_value = lax.psum(jnp.sum(log_ratio), 'blk') / whole_count  177 us
    all_gather x1, waiting for transfers between devices, body(): lax.all_gather(reference_samples, 'blk', axis=0, tiled=True)  176 us
    dot_general x1, matrix products, fold(): products = jnp.dot(pool_rows, joined.T, preferred_element_type=jnp.float32)  23.1 us
    all_to_all x1, starting transfers between devices, body(): lax.all_to_all(jnp.stack([target_samples] * lax.axis_size('blk')), 'blk',...  14.4 us
  transfers between devices with their start and end apart: 2, of which 1 were waited for; matrix products, arithmetic and copies ran while one was open for 1% of the time, Pallas kernels for 0%

profile of v1, /device:TPU:32, one launch (start us, length us, event | category | flops | bytes accessed | tf_op | source)
XLA Modules:
  0.0 640.7 jit_solution(7529540277689439377)
XLA Ops:
  7.2 0.0 copy-start.1
  7.2 0.0 all-gather.2.cloned.1.call-start
  7.2 0.7 all-gather.2.cloned.1.call-update
  7.9 4.3 stack.2
  12.2 14.4 %all-to-all-start = ((bf16[64,64,768]{2,1,0:T(8,128)(2,1)}), bf16[64,64,768]{2,1,0:T(8,128)(2,1)}, u32[]{:S(2)}, u32[]{:S(2)}) async-start(bf16[64,64,768]{2,1,0:T(8,128)(2,1)} %stack.2), calls=%async_computation | async-start | bytes 12582912 | tf_op jit(solution)/shard_map/all_to_all | solution.py:46
  26.6 0.0 copy-done.1
  26.6 0.4 multiply_reduce_fusion.1
  27.0 175.8 %all-gather.2.cloned.1.call-done = bf16[4096,768]{1,0:T(8,128)(2,1)} async-done(((bf16[64,768]{1,0:T(8,128)(2,1)}), bf16[4096,768]{1,0:T(8,128)(2,1)}) %all-gather.2.cloned.1.call-update) | async-done | bytes 6291472 | tf_op jit(solution)/shard_map/all_gather | solution.py:49
  202.8 0.0 all-to-all-done
  202.8 9.5 %multiply_reduce_fusion = f32[8192]{0:T(1024)S(1)} fusion(bf16[4096,768]{1,0:T(8,128)(2,1)} %all-gather.2.cloned.1.call-done, bf16[4096,768]{1,0:T(8,128)(2,1)} %bitcast), kind=kLoop, calls=%fused_computation.1 | loop fusion | flops 37740544 | bytes 12615680 | tf_op jit(solution)/shard_map/reduce_sum | solution.py:16
  212.3 23.1 %multiply_bitcast_fusion = f32[1024,8192]{0,1:T(8,128)} fusion(bf16[1024,768]{1,0:T(8,128)(2,1)S(1)} %copy-done.1, f32[8192]{0:T(1024)S(1)} %multiply_reduce_fusion, f32[1024]{0:T(1024)S(1)} %multiply_reduce_fusion.1, bf16[4096,768]{1,0:T(8,128)(2,1)} %all-gather.2.cloned.1.call-done, bf16[4096,768]{1,0:T(8,128)(2,1)} %bitcast), kind=kOutput, calls=%fused_computation | convolution fusion | flops 12943622144 | bytes 47747072 | tf_op jit(solution)/shard_map/dot_general | solution.py:17
  235.4 0.0 copy-start
  235.4 11.7 %slice_reduce_fusion.1 = (f32[1024]{0:T(1024)S(1)}, f32[1024]{0:T(1024)S(1)}) fusion(f32[1024,8192]{0,1:T(8,128)} %multiply_bitcast_fusion), kind=kLoop, calls=%fused_computation.5 | loop fusion | flops 8386560 | bytes 33562624 | tf_op jit(solution)/shard_map/reduce_max | solution.py:24
  247.2 8.6 %copy-done = f32[1024,8192]{0,1:T(8,128)S(1)} copy-done((f32[1024,8192]{0,1:T(8,128)S(1)}, f32[1024,8192]{0,1:T(8,128)}, u32[]{:S(2)}) %copy-start) | copy-done | bytes 33554456
  255.7 4.5 exponential_reduce_fusion.1
  260.2 6.1 all-reduce.1
  266.3 5.9 all-reduce
  272.2 0.6 fusion.1
  272.8 0.0 copy-start.2
  272.8 176.7 %psum.30 = f32[]{:T(128)} all-reduce(f32[]{:T(128)} %get-tuple-element.10), channel_id=1, replica_groups=mesh['blk'=64,'row'=4] {'blk'}, use_global_device_ids=true, to_apply=%region_11.0 | all-reduce | flops 1 | bytes 8 | tf_op jit(solution)/shard_map/psum | solution.py:59
  450.1 0.6 multiply_reduce_fusion.2
  450.7 181.8 %psum.31 = f32[]{:T(128)} all-reduce(f32[]{:T(128)} %multiply_reduce_fusion.2), channel_id=1, replica_groups=mesh['blk'=64,'row'=4] {'blk'}, use_global_device_ids=true, to_apply=%region_13.0 | all-reduce | flops 1 | bytes 8 | tf_op jit(solution)/shard_map/psum | solution.py:60
  633.3 0.6 subtract_divide_fusion
  633.9 0.0 copy-done.2
  (3 shorter events, 0.0 us)
Async XLA Ops:
  7.2 19.5 %copy-start.1 = (bf16[1024,768]{1,0:T(8,128)(2,1)S(1)}, bf16[1024,768]{1,0:T(8,128)(2,1)}, u32[]{:S(2)}) copy-start(bf16[1024,768]{1,0:T(8,128)(2,1)} %param.3) | copy-start | bytes 4718596
  7.2 195.6 %all-gather.2.cloned.1.call-start = ((), (), s32[]{:S(2)}) async-start(), calls=%async_computation.1 | async-start | bytes 6389760 | tf_op jit(solution)/shard_map/all_gather | solution.py:49
  12.2 190.6 %all-to-all-start = ((bf16[64,64,768]{2,1,0:T(8,128)(2,1)}), bf16[64,64,768]{2,1,0:T(8,128)(2,1)}, u32[]{:S(2)}, u32[]{:S(2)}) async-start(bf16[64,64,768]{2,1,0:T(8,128)(2,1)} %stack.2), calls=%async_computation | async-start | bytes 12582912 | tf_op jit(solution)/shard_map/all_to_all | solution.py:46
  235.4 20.3 %copy-start = (f32[1024,8192]{0,1:T(8,128)S(1)}, f32[1024,8192]{0,1:T(8,128)}, u32[]{:S(2)}) copy-start(f32[1024,8192]{0,1:T(8,128)} %multiply_bitcast_fusion) | copy-start | bytes 100663296
  272.8 361.1 %copy-start.2 = (f32[1024]{0:T(1024)}, f32[1024]{0:T(1024)S(1)}, u32[]{:S(2)}) copy-start(f32[1024]{0:T(1024)S(1)} %get-tuple-element.11) | copy-start | bytes 12292
Sparse Core Ops, SparseCore 0:
  11.7 191.1 all-gather.1
